TPU v7x, 128 devices: a whole 4x4x4 slice. The times are simulated.
128 devices in a mesh: fsdp: 16 (over z, y), tensor: 8 (over x, core).
Axes of the slice: x: 4, y: 4, z: 4, core: 2. Of those that a mesh axis runs over, the one named last changes fastest.
Arguments:
- grad_blocks: bfloat16 [2, 16896, 1536], P(None, 'tensor', 'fsdp'), may hold values from -150 to 150
- master_shard: float32 [2, 16896, 1536], P(None, ('fsdp', 'tensor')), may hold values from -6 to 6
- first_moment: float32 [2, 16896, 1536], P(None, ('fsdp', 'tensor')), may hold values from -2 to 2
- second_moment: float32 [2, 16896, 1536], P(None, ('fsdp', 'tensor')), may hold values from 0.05 to 0.5
- average_shard: float32 [2, 16896, 1536], P(None, ('tensor', 'fsdp')), may hold values from -6 to 6
- gain_grads: bfloat16 [2, 3072], P(None, ('fsdp', 'tensor')), may hold values from -24 to 24
- gain_master: float32 [2, 3072], P(None, ('fsdp', 'tensor')), may hold values from 0.5 to 1.5
- gain_first: float32 [2, 3072], P(None, ('fsdp', 'tensor')), may hold values from -2 to 2
- gain_second: float32 [2, 3072], P(None, ('fsdp', 'tensor')), may hold values from 0.05 to 0.5
- gain_average: float32 [2, 3072], P(None, ('fsdp', 'tensor')), may hold values from 0.5 to 1.5
Outputs:
- train_weights: bfloat16 [2, 16896, 1536], P(None, 'tensor', 'fsdp')
- master_next: float32 [2, 16896, 1536], P(None, ('fsdp', 'tensor'))
- first_next: float32 [2, 16896, 1536], P(None, ('fsdp', 'tensor'))
- second_next: float32 [2, 16896, 1536], P(None, ('fsdp', 'tensor'))
- average_next: float32 [2, 16896, 1536], P(None, ('tensor', 'fsdp'))
- gain_weights: bfloat16 [2, 3072], replicated
- master_gains: float32 [2, 3072], P(None, ('fsdp', 'tensor'))
- first_gains: float32 [2, 3072], P(None, ('fsdp', 'tensor'))
- second_gains: float32 [2, 3072], P(None, ('fsdp', 'tensor'))
- average_gains: float32 [2, 3072], P(None, ('fsdp', 'tensor'))
All inputs are finite; a program needn't handle non-finite values.
Results may differ from a plain program's by a relative error of at most 0.001.
Values may be sent and summed in bfloat16 or wider, within the bound.
A program may use at most 128 MiB of HBM per device.

v0:
```python
import jax
import jax.numpy as jnp
from jax import lax
from jax.sharding import PartitionSpec as P

STEP = 20
learn_rate = 0.1
weight_decay = 0.1
beta_first = 0.9
beta_second = 0.95
adam_epsilon = 1e-08
average_decay = 0.9
clip_level = 0.5
mean_epsilon = 1e-06


def adam_step(gradient, master, first_state, second_state, clip_scale):
    clipped = gradient.astype(jnp.float32) * clip_scale
    first_new = beta_first * first_state + (1.0 - beta_first) * clipped
    second_new = beta_second * second_state + (1.0 - beta_second) * clipped * clipped
    first_fix = 1.0 - beta_first**STEP
    second_fix = 1.0 - beta_second**STEP
    direction = (
        first_new / first_fix / (jnp.sqrt(second_new / second_fix) + adam_epsilon)
        + weight_decay * master
    )
    master_new = master - learn_rate * direction
    return (master_new, first_new, second_new)


def on_device(
    grad_blocks,
    master_shard,
    first_moment,
    second_moment,
    average_shard,
    gain_grads,
    gain_master,
    gain_first,
    gain_second,
    gain_average,
):
    fsdp_count = lax.axis_size("fsdp")
    tensor_count = lax.axis_size("tensor")
    group_ratio = fsdp_count // tensor_count
    layer_count, block_rows, block_cols = grad_blocks.shape
    shard_rows = block_rows // fsdp_count
    width_full = block_cols * fsdp_count
    entries = (grad_blocks.size + gain_grads.size) * fsdp_count * tensor_count
    gain_wide = gain_grads.astype(jnp.float32)
    gain_squares = jnp.sum(gain_wide * gain_wide)
    sectioned = grad_blocks.reshape(layer_count, group_ratio, tensor_count, shard_rows, block_cols)
    arrived = lax.all_to_all(
        lax.all_to_all(sectioned, "tensor", split_axis=2, concat_axis=1, tiled=True),
        "fsdp",
        split_axis=1,
        concat_axis=4,
        tiled=True,
    )
    flat_grads = arrived.reshape(layer_count, shard_rows, width_full)
    flat_wide = flat_grads.astype(jnp.float32)
    total_squares = lax.psum(jnp.sum(flat_wide * flat_wide) + gain_squares, ("fsdp", "tensor"))
    clip_scale = jnp.minimum(1.0, clip_level / jnp.sqrt(total_squares / entries + mean_epsilon))
    master_next, first_next, second_next = adam_step(
        flat_grads, master_shard, first_moment, second_moment, clip_scale
    )
    master_gains, first_gains, second_gains = adam_step(
        gain_grads, gain_master, gain_first, gain_second, clip_scale
    )
    average_gains = average_decay * gain_average + (1.0 - average_decay) * master_gains
    outgoing = master_next.reshape(layer_count, 1, 1, shard_rows, width_full)
    home_float = lax.all_to_all(
        lax.all_to_all(
            outgoing.astype(jnp.bfloat16), "fsdp", split_axis=4, concat_axis=1, tiled=True
        ),
        "tensor",
        split_axis=1,
        concat_axis=2,
        tiled=True,
    ).astype(outgoing.dtype)
    train_float = home_float.reshape(layer_count, block_rows, block_cols)
    train_weights = train_float.astype(jnp.bfloat16)
    sorted_rows = train_float.reshape(layer_count, fsdp_count, shard_rows, block_cols)
    average_rows = lax.all_to_all(
        sorted_rows.astype(jnp.bfloat16), "fsdp", split_axis=1, concat_axis=3, tiled=True
    ).astype(sorted_rows.dtype)
    average_layout = average_rows.reshape(layer_count, shard_rows, width_full)
    average_next = average_decay * average_shard + (1.0 - average_decay) * average_layout
    gain_weights = lax.all_gather(
        master_gains.astype(jnp.bfloat16), ("fsdp", "tensor"), axis=1, tiled=True
    )
    return (
        train_weights,
        master_next,
        first_next,
        second_next,
        average_next,
        gain_weights,
        master_gains,
        first_gains,
        second_gains,
        average_gains,
    )


def solution(mesh):
    placed = (
        P(None, "tensor", "fsdp"),
        P(None, ("fsdp", "tensor"), None),
        P(None, ("fsdp", "tensor"), None),
        P(None, ("fsdp", "tensor"), None),
        P(None, ("tensor", "fsdp"), None),
        P(None, ("fsdp", "tensor")),
        P(None, ("fsdp", "tensor")),
        P(None, ("fsdp", "tensor")),
        P(None, ("fsdp", "tensor")),
        P(None, ("fsdp", "tensor")),
    )
    return jax.shard_map(
        on_device,
        mesh=mesh,
        in_specs=placed,
        out_specs=(
            P(None, "tensor", "fsdp"),
            P(None, ("fsdp", "tensor"), None),
            P(None, ("fsdp", "tensor"), None),
            P(None, ("fsdp", "tensor"), None),
            P(None, ("tensor", "fsdp"), None),
            P(),
            P(None, ("fsdp", "tensor")),
            P(None, ("fsdp", "tensor")),
            P(None, ("fsdp", "tensor")),
            P(None, ("fsdp", "tensor")),
        ),
        check_vma=False,
    )
```

profile of v0, /device:TPU:1, one launch (start us, length us, event | category | flops | bytes accessed | tf_op | source)
XLA Modules:
  0.0 253.8 jit_solution(17145453859018370600)
XLA Ops:
  0.6 5.4 %reshape.52 = bf16[2,2,8,132,96]{3,2,1,4,0:T(8,128)(2,1)S(1)} reshape(bf16[2,2112,96]{1,2,0:T(8,128)(2,1)} %param.10) | data formatting | bytes 1622016 | tf_op jit(solution)/shard_map/reshape | solution.py:52
  6.0 2.1 copy.92
  8.1 21.5 %all_to_all.75 = bf16[2,2,8,132,96]{4,1,3,0,2:T(2,128)(2,1)S(1)} all-to-all(bf16[2,2,8,132,96]{4,1,3,0,2:T(2,128)(2,1)S(1)} %copy.92), channel_id=1, replica_groups=mesh['fsdp'=16,'tensor'=8] {'tensor'}, dimensions={2} | all-to-all | bytes 1622016 | tf_op jit(solution)/shard_map/all_to_all | solution.py:54
  29.6 0.7 copy.93
  30.3 0.0 copy-start.6
  30.4 2.1 copy.94
  32.5 7.8 %all-to-all-start.1 = ((bf16[2,16,1,132,96]{4,0,3,2,1:T(2,128)(2,1)}), bf16[2,16,1,132,96]{4,0,3,2,1:T(2,128)(2,1)S(1)}, u32[]{:S(2)}, u32[]{:S(2)}) async-start(bf16[2,16,1,132,96]{4,0,3,2,1:T(2,128)(2,1)} %copy.94), calls=%async_computation.1 | async-start | bytes 2162688 | tf_op jit(solution)/shard_map/all_to_all | solution.py:53
  40.2 0.0 copy-done.6
  40.2 0.6 fusion.7
  40.8 15.9 %all-to-all-done.1 = bf16[2,16,1,132,96]{4,0,3,2,1:T(2,128)(2,1)S(1)} async-done(((bf16[2,16,1,132,96]{4,0,3,2,1:T(2,128)(2,1)}), bf16[2,16,1,132,96]{4,0,3,2,1:T(2,128)(2,1)S(1)}, u32[]{:S(2)}, u32[]{:S(2)}) %all-to-all-start.1) | async-done | bytes 811040 | tf_op jit(solution)/shard_map/all_to_all | solution.py:53
  56.7 2.8 %fusion = f32[]{:T(128)} fusion(bf16[2,16,1,132,96]{4,0,3,2,1:T(2,128)(2,1)S(1)} %all-to-all-done.1), kind=kLoop, calls=%fused_computation.3 | loop fusion | flops 1216511 | bytes 811012 | tf_op jit(solution)/shard_map/reduce_sum | solution.py:62
  60.8 64.4 %psum.7 = f32[]{:T(128)} all-reduce(f32[]{:T(128)S(6)} %add.44), channel_id=1, replica_groups=mesh['fsdp'=16,'tensor'=8] {'fsdp','tensor'}, use_global_device_ids=true, to_apply=%region_2.0 | all-reduce | flops 1 | bytes 8 | tf_op jit(solution)/shard_map/psum | solution.py:62
  125.9 0.7 fusion.1
  126.7 0.4 copy.95
  127.1 2.3 mul.112
  129.4 6.5 %convert_bitcast_fusion = (bf16[2,1,1,132,1536]{4,3,0,2,1:T(8,128)(2,1)}, f32[2,132,1536]{2,1,0:T(8,128)}, f32[2,132,1536]{2,1,0:T(8,128)}, f32[2,132,1536]{2,1,0:T(8,128)S(1)}) fusion(f32[2,132,1536]{2,0,1:T(2,128)} %param.11, f32[2,132,1536]{2,1,0:T(8,128)} %mul.112, f32[2,132,1536]{2,0,1:T(2,128)} %param.12, f32[2,132,1536]{2,0,1:T(2,128)} %param.13), kind=kLoop, calls=%fused_computation.14 | loop fusion | flops 6488064 | bytes 12165120 | tf_op jit(solution)/shard_map/convert_element_type | solution.py:74
  135.9 3.5 %copy.99 = bf16[2,1,1,132,1536]{3,0,2,1,4:T(2,128)(2,1)S(1)} copy(bf16[2,1,1,132,1536]{4,3,0,2,1:T(8,128)(2,1)} %get-tuple-element.74) | data formatting | bytes 1622016 | tf_op jit(solution)/shard_map/convert_element_type | solution.py:74
  139.5 25.4 %all_to_all.76 = bf16[2,1,1,132,1536]{3,0,2,1,4:T(2,128)(2,1)} all-to-all(bf16[2,1,1,132,1536]{3,0,2,1,4:T(2,128)(2,1)S(1)} %copy.99), channel_id=1, replica_groups=mesh['fsdp'=16,'tensor'=8] {'fsdp'}, dimensions={4} | all-to-all | bytes 1622016 | tf_op jit(solution)/shard_map/all_to_all | solution.py:73
  164.9 3.5 %copy.116 = bf16[2,1,1,132,16,96]{5,4,3,0,2,1:T(8,128)(2,1)S(1)} copy(bf16[2,1,1,132,16,96]{3,0,5,4,2,1:T(2,128)(2,1)} %bitcast.47) | data formatting | bytes 1622016 | tf_op jit(solution)/shard_map/all_to_all | solution.py:73
  168.4 1.1 copy.101
  169.5 20.2 %all_to_all.77 = bf16[2,16,1,132,96]{4,0,3,2,1:T(2,128)(2,1)S(1)} all-to-all(bf16[2,16,1,132,96]{4,0,3,2,1:T(2,128)(2,1)S(1)} %copy.101), channel_id=1, replica_groups=mesh['fsdp'=16,'tensor'=8] {'tensor'}, dimensions={1} | all-to-all | bytes 1622016 | tf_op jit(solution)/shard_map/all_to_all | solution.py:72
  189.7 0.1 copy.102
  189.8 0.1 copy.133
  190.0 2.1 copy.106
  192.1 4.6 %all-to-all-start.4 = ((bf16[2,16,132,96]{3,0,2,1:T(2,128)(2,1)}), bf16[2,16,132,96]{3,0,2,1:T(2,128)(2,1)}, u32[]{:S(2)}, u32[]{:S(2)}) async-start(bf16[2,16,132,96]{3,0,2,1:T(2,128)(2,1)} %copy.106), calls=%async_computation.4 | async-start | bytes 2162688 | tf_op jit(solution)/shard_map/all_to_all | solution.py:84
  196.7 0.0 copy-start
  196.7 4.0 %copy.110 = f32[2,132,1536]{2,0,1:T(2,128)} copy(f32[2,132,1536]{2,1,0:T(8,128)} %get-tuple-element.75) | data formatting | bytes 3244032
  200.7 0.0 copy-done
  200.7 2.4 copy.111
  203.1 0.0 copy-start.1
  203.1 0.0 copy-start.2
  203.1 0.0 copy-start.3
  203.1 0.0 copy-start.4
  203.1 2.4 copy.112
  205.5 0.0 copy-done.1
  205.5 0.0 copy-done.2
  205.5 0.0 copy-done.3
  205.5 0.0 copy-done.4
  205.5 0.6 multiply_add_fusion
  206.1 0.0 copy-start.5
  206.1 31.2 %all-gather = bf16[128,24,2]{1,2,0:T(2,128)(2,1)S(1)} all-gather(bf16[1,24,2]{1,2,0:T(2,128)(2,1)S(1)} %convert_bitcast_fusion.1), channel_id=1, replica_groups=mesh['fsdp'=16,'tensor'=8] {'fsdp','tensor'}, dimensions={0}, use_global_device_ids=true | all-gather | bytes 12384 | tf_op jit(solution)/shard_map/all_gather | solution.py:89
  237.4 0.7 reshape.51
  238.1 3.0 %copy.117 = bf16[2,2,8,1,132,96]{4,2,1,5,0,3:T(8,128)(2,1)S(1)} copy(bf16[2,2,8,1,132,96]{5,1,2,4,0,3:T(2,128)(2,1)S(1)} %bitcast.46) | data formatting | bytes 1622016
  241.1 2.9 %reshape.53 = bf16[2,2112,96]{1,2,0:T(8,128)(2,1)} reshape(bf16[2,2,8,1,132,96]{4,2,1,5,0,3:T(8,128)(2,1)S(1)} %copy.117) | data formatting | bytes 1622016
  244.0 0.0 copy-done.5
  244.0 0.0 all-to-all-done.4
  244.0 2.4 multiply_bitcast_fusion
  246.3 0.4 copy.107
  246.8 2.3 mul.125
  249.1 2.4 fusion.3
  251.4 2.4 copy.113
  (2 shorter events, 0.0 us)
Async XLA Ops:
  30.3 9.9 %copy-start.6 = (bf16[2,24]{1,0:T(2,128)(2,1)S(1)}, bf16[2,24]{1,0:T(2,128)(2,1)}, u32[]{:S(2)}) copy-start(bf16[2,24]{1,0:T(2,128)(2,1)} %param.15) | copy-start | bytes 292
  32.5 24.2 %all-to-all-start.1 = ((bf16[2,16,1,132,96]{4,0,3,2,1:T(2,128)(2,1)}), bf16[2,16,1,132,96]{4,0,3,2,1:T(2,128)(2,1)S(1)}, u32[]{:S(2)}, u32[]{:S(2)}) async-start(bf16[2,16,1,132,96]{4,0,3,2,1:T(2,128)(2,1)} %copy.94), calls=%async_computation.1 | async-start | bytes 2162688 | tf_op jit(solution)/shard_map/all_to_all | solution.py:53
  192.1 51.9 %all-to-all-start.4 = ((bf16[2,16,132,96]{3,0,2,1:T(2,128)(2,1)}), bf16[2,16,132,96]{3,0,2,1:T(2,128)(2,1)}, u32[]{:S(2)}, u32[]{:S(2)}) async-start(bf16[2,16,132,96]{3,0,2,1:T(2,128)(2,1)} %copy.106), calls=%async_computation.4 | async-start | bytes 2162688 | tf_op jit(solution)/shard_map/all_to_all | solution.py:84
  196.7 4.0 %copy-start = (f32[2,132,1536]{2,1,0:T(8,128)S(1)}, f32[2,132,1536]{2,1,0:T(8,128)}, u32[]{:S(2)}) copy-start(f32[2,132,1536]{2,1,0:T(8,128)} %get-tuple-element.76) | copy-start | bytes 4866052
  203.1 2.4 copy-start.1
  203.1 2.4 copy-start.2
  203.1 2.4 copy-start.3
  203.1 2.4 copy-start.4
  206.1 37.9 %copy-start.5 = (f32[2,24]{1,0:T(2,128)}, f32[2,24]{1,0:T(2,128)S(1)}, u32[]{:S(2)}) copy-start(f32[2,24]{1,0:T(2,128)S(1)} %get-tuple-element.71) | copy-start | bytes 580
where the time goes:
time: 255 us; the launch traced here: 254 us
  blocking collectives  163 us (64%)
  local copies, waits for them, and re-layouts  44 us (17%)
  other arithmetic  16 us (6%)
  waiting for transfers between devices  15.9 us (6%)
  starting transfers between devices  12.4 us (5%)
  between operations  2.8 us (1%)
    psum x1, blocking collectives, on_device(): lax.psum(jnp.sum(flat_wide * flat_wide) + gain_squares, ('fsdp', 'tensor'))  64.4 us
    all_gather x1, blocking collectives, on_device(): lax.all_gather(master_gains.astype(jnp.bfloat16), ('fsdp', 'tensor'), axi...  31.2 us
    all_to_all x1, blocking collectives, on_device(): lax.all_to_all(outgoing.astype(jnp.bfloat16), 'fsdp', split_axis=4, conca...  25.4 us
    all_to_all x1, blocking collectives, on_device(): lax.all_to_all(sectioned, 'tensor', split_axis=2, concat_axis=1, tiled=True)  21.5 us
    all_to_all x1, blocking collectives, on_device(): lax.all_to_all(lax.all_to_all(outgoing.astype(jnp.bfloat16), 'fsdp', spli...  20.2 us
    unnamed x21, local copies, waits for them, and re-layouts  17.9 us
    all_to_all x1, waiting for transfers between devices, on_device(): lax.all_to_all(lax.all_to_all(sectioned, 'tensor', split_axis=2, concat_a...  15.9 us
    all_to_all x1, starting transfers between devices, on_device(): lax.all_to_all(lax.all_to_all(sectioned, 'tensor', split_axis=2, concat_a...  7.77 us
  transfers between devices with their start and end apart: 2, of which 1 were waited for; matrix products, arithmetic and copies ran while one was open for 7% of the time, Pallas kernels for 0%

commit v1 on v0

--- a/solution.py
+++ b/solution.py
@@ -86,8 +86,14 @@
     ).astype(sorted_rows.dtype)
     average_layout = average_rows.reshape(layer_count, shard_rows, width_full)
     average_next = average_decay * average_shard + (1.0 - average_decay) * average_layout
-    gain_weights = lax.all_gather(
-        master_gains.astype(jnp.bfloat16), ("fsdp", "tensor"), axis=1, tiled=True
+    gain_weights = jnp.concatenate(
+        lax.all_to_all(
+            jnp.stack([master_gains.astype(jnp.bfloat16)] * lax.axis_size(("fsdp", "tensor"))),
+            ("fsdp", "tensor"),
+            0,
+            0,
+        ),
+        axis=1,
     )
     return (
         train_weights,

time: 255 us -> 239 us (0.937)
  blocking collectives: 163 us -> 111 us
  waiting for transfers between devices: 15.9 us -> 37.6 us
  starting transfers between devices: 12.4 us -> 22 us
  local copies, waits for them, and re-layouts: 44 us -> 47.3 us
    all_gather x1 -> x0, blocking collectives: 31.2 us -> none  [on_device(): lax.all_gather(master_gains.astype(jnp.bfloat16), ('fsdp', 'tensor'), axi...]
    all_to_all x0 -> x2, waiting for transfers between devices: none -> 20.9 us  [the longest x1 14.8 us: on_device(): lax.all_to_all(lax.all_to_all(outgoing.astype(jnp.bfloat16), 'fsdp', spli...]
    all_to_all x1 -> x0, blocking collectives: 20.2 us -> none  [on_device(): lax.all_to_all(lax.all_to_all(outgoing.astype(jnp.bfloat16), 'fsdp', spli...]
    all_to_all x0 -> x2, starting transfers between devices: none -> 9.62 us  [the longest x1 5.37 us: on_device(): lax.all_to_all(lax.all_to_all(outgoing.astype(jnp.bfloat16), 'fsdp', spli...]
    unnamed x21 -> x22, local copies, waits for them, and re-layouts: 17.9 us -> 17.4 us
  transfers between devices with their start and end apart: 2 -> 4, of which waited for: 1 -> 4; matrix products, arithmetic and copies ran while one was open for 7% -> 9% of each run, Pallas kernels for 0% -> 0%
where the time goes in v1:
time: 239 us; the launch traced here: 237 us
  blocking collectives  111 us (46%)
  local copies, waits for them, and re-layouts  47.3 us (20%)
  waiting for transfers between devices  37.6 us (16%)
  starting transfers between devices  22 us (9%)
  other arithmetic  16 us (7%)
  between operations  2.84 us (1%)
    psum x1, blocking collectives, on_device(): lax.psum(jnp.sum(flat_wide * flat_wide) + gain_squares, ('fsdp', 'tensor'))  64.4 us
    all_to_all x1, blocking collectives, on_device(): lax.all_to_all(outgoing.astype(jnp.bfloat16), 'fsdp', split_axis=4, conca...  25.4 us
    all_to_all x1, blocking collectives, on_device(): lax.all_to_all(sectioned, 'tensor', split_axis=2, concat_axis=1, tiled=True)  21.5 us
    unnamed x22, local copies, waits for them, and re-layouts  17.4 us
    all_to_all x1, waiting for transfers between devices, on_device(): lax.all_to_all(lax.all_to_all(sectioned, 'tensor', split_axis=2, concat_a...  15.9 us
    all_to_all x1, waiting for transfers between devices, on_device(): lax.all_to_all(lax.all_to_all(outgoing.astype(jnp.bfloat16), 'fsdp', spli...  14.8 us
    all_to_all x1, starting transfers between devices, on_device(): lax.all_to_all(lax.all_to_all(sectioned, 'tensor', split_axis=2, concat_a...  7.77 us
    reshape x2, local copies, waits for them, and re-layouts, on_device(): grad_blocks.reshape(layer_count, group_ratio, tensor_count, shard_rows, b...  7.46 us
  transfers between devices with their start and end apart: 4, of which 4 were waited for; matrix products, arithmetic and copies ran while one was open for 9% of the time, Pallas kernels for 0%

profile of v1, /device:TPU:1, one launch (start us, length us, event | category | flops | bytes accessed | tf_op | source)
XLA Modules:
  0.0 237.1 jit_solution(8874222611382244536)
XLA Ops:
  0.6 5.4 %reshape.60 = bf16[2,2,8,132,96]{3,2,1,4,0:T(8,128)(2,1)S(1)} reshape(bf16[2,2112,96]{1,2,0:T(8,128)(2,1)} %param.10) | data formatting | bytes 1622016 | tf_op jit(solution)/shard_map/reshape | solution.py:52
  6.0 2.1 copy.88
  8.1 21.5 %all_to_all.80 = bf16[2,2,8,132,96]{4,1,3,0,2:T(2,128)(2,1)S(1)} all-to-all(bf16[2,2,8,132,96]{4,1,3,0,2:T(2,128)(2,1)S(1)} %copy.88), channel_id=1, replica_groups=mesh['fsdp'=16,'tensor'=8] {'tensor'}, dimensions={2} | all-to-all | bytes 1622016 | tf_op jit(solution)/shard_map/all_to_all | solution.py:54
  29.6 0.7 copy.89
  30.3 0.0 copy-start.7
  30.4 2.1 copy.90
  32.5 7.8 %all-to-all-start.1 = ((bf16[2,16,1,132,96]{4,0,3,2,1:T(2,128)(2,1)}), bf16[2,16,1,132,96]{4,0,3,2,1:T(2,128)(2,1)S(1)}, u32[]{:S(2)}, u32[]{:S(2)}) async-start(bf16[2,16,1,132,96]{4,0,3,2,1:T(2,128)(2,1)} %copy.90), calls=%async_computation.1 | async-start | bytes 2162688 | tf_op jit(solution)/shard_map/all_to_all | solution.py:53
  40.2 0.0 copy-done.7
  40.2 0.6 fusion.7
  40.8 15.9 %all-to-all-done.1 = bf16[2,16,1,132,96]{4,0,3,2,1:T(2,128)(2,1)S(1)} async-done(((bf16[2,16,1,132,96]{4,0,3,2,1:T(2,128)(2,1)}), bf16[2,16,1,132,96]{4,0,3,2,1:T(2,128)(2,1)S(1)}, u32[]{:S(2)}, u32[]{:S(2)}) %all-to-all-start.1) | async-done | bytes 811040 | tf_op jit(solution)/shard_map/all_to_all | solution.py:53
  56.7 2.8 %fusion = f32[]{:T(128)} fusion(bf16[2,16,1,132,96]{4,0,3,2,1:T(2,128)(2,1)S(1)} %all-to-all-done.1), kind=kLoop, calls=%fused_computation.3 | loop fusion | flops 1216511 | bytes 811012 | tf_op jit(solution)/shard_map/reduce_sum | solution.py:62
  60.8 64.4 %psum.7 = f32[]{:T(128)} all-reduce(f32[]{:T(128)S(6)} %add.44), channel_id=1, replica_groups=mesh['fsdp'=16,'tensor'=8] {'fsdp','tensor'}, use_global_device_ids=true, to_apply=%region_2.0 | all-reduce | flops 1 | bytes 8 | tf_op jit(solution)/shard_map/psum | solution.py:62
  126.0 0.7 fusion.1
  126.7 0.4 copy.91
  127.1 2.3 mul.112
  129.4 6.5 %convert_bitcast_fusion = (bf16[2,1,1,132,1536]{4,3,0,2,1:T(8,128)(2,1)}, f32[2,132,1536]{2,1,0:T(8,128)}, f32[2,132,1536]{2,1,0:T(8,128)}, f32[2,132,1536]{2,1,0:T(8,128)S(1)}) fusion(f32[2,132,1536]{2,0,1:T(2,128)} %param.11, f32[2,132,1536]{2,1,0:T(8,128)} %mul.112, f32[2,132,1536]{2,0,1:T(2,128)} %param.12, f32[2,132,1536]{2,0,1:T(2,128)} %param.13), kind=kLoop, calls=%fused_computation.14 | loop fusion | flops 6488064 | bytes 12165120 | tf_op jit(solution)/shard_map/convert_element_type | solution.py:74
  135.9 3.5 %copy.95 = bf16[2,1,1,132,1536]{3,0,2,1,4:T(2,128)(2,1)S(1)} copy(bf16[2,1,1,132,1536]{4,3,0,2,1:T(8,128)(2,1)} %get-tuple-element.74) | data formatting | bytes 1622016 | tf_op jit(solution)/shard_map/convert_element_type | solution.py:74
  139.4 25.4 %all_to_all.81 = bf16[2,1,1,132,1536]{3,0,2,1,4:T(2,128)(2,1)} all-to-all(bf16[2,1,1,132,1536]{3,0,2,1,4:T(2,128)(2,1)S(1)} %copy.95), channel_id=1, replica_groups=mesh['fsdp'=16,'tensor'=8] {'fsdp'}, dimensions={4} | all-to-all | bytes 1622016 | tf_op jit(solution)/shard_map/all_to_all | solution.py:73
  164.9 3.5 %copy.112 = bf16[2,1,1,132,16,96]{5,4,3,0,2,1:T(8,128)(2,1)S(1)} copy(bf16[2,1,1,132,16,96]{3,0,5,4,2,1:T(2,128)(2,1)} %bitcast.41) | data formatting | bytes 1622016 | tf_op jit(solution)/shard_map/all_to_all | solution.py:73
  168.4 0.0 copy-start.2
  168.4 0.0 copy-start.3
  168.4 0.0 copy-start.4
  168.4 0.0 copy-start.5
  168.4 2.1 copy.97
  170.5 5.4 %all-to-all-start.3 = ((bf16[2,16,1,132,96]{4,0,3,2,1:T(2,128)(2,1)}), bf16[2,16,1,132,96]{4,0,3,2,1:T(2,128)(2,1)S(1)}, u32[]{:S(2)}, u32[]{:S(2)}) async-start(bf16[2,16,1,132,96]{4,0,3,2,1:T(2,128)(2,1)} %copy.97), calls=%async_computation.3 | async-start | bytes 2162688 | tf_op jit(solution)/shard_map/all_to_all | solution.py:72
  175.9 0.0 copy-done.2
  175.9 0.0 copy-done.3
  175.9 0.0 copy-done.4
  175.9 0.0 copy-done.5
  175.9 0.6 multiply_add_fusion
  176.5 0.0 copy-start.6
  176.5 14.8 %all-to-all-done.3 = bf16[2,16,1,132,96]{4,0,3,2,1:T(2,128)(2,1)S(1)} async-done(((bf16[2,16,1,132,96]{4,0,3,2,1:T(2,128)(2,1)}), bf16[2,16,1,132,96]{4,0,3,2,1:T(2,128)(2,1)S(1)}, u32[]{:S(2)}, u32[]{:S(2)}) %all-to-all-start.3) | async-done | bytes 811040 | tf_op jit(solution)/shard_map/all_to_all | solution.py:72
  191.4 0.0 copy-start.1
  191.4 0.7 stack.2
  192.1 0.3 copy-done.1
  192.4 4.3 %all-to-all-start.5 = ((bf16[128,2,24]{2,1,0:T(2,128)(2,1)}), bf16[128,2,24]{2,1,0:T(2,128)(2,1)S(1)}, u32[]{:S(2)}, u32[]{:S(2)}) async-start(bf16[128,2,24]{2,1,0:T(2,128)(2,1)} %stack.2), calls=%async_computation.5 | async-start | bytes 131072 | tf_op jit(solution)/shard_map/all_to_all | solution.py:90
  196.6 1.4 copy.98
  198.0 0.1 copy.129
  198.2 0.0 copy-done.6
  198.2 2.1 copy.102
  200.3 6.0 %all-to-all-done.5 = bf16[128,2,24]{2,1,0:T(2,128)(2,1)S(1)} async-done(((bf16[128,2,24]{2,1,0:T(2,128)(2,1)}), bf16[128,2,24]{2,1,0:T(2,128)(2,1)S(1)}, u32[]{:S(2)}, u32[]{:S(2)}) %all-to-all-start.5) | async-done | bytes 12320 | tf_op jit(solution)/shard_map/all_to_all | solution.py:90
  206.3 4.6 %all-to-all-start.4 = ((bf16[2,16,132,96]{3,0,2,1:T(2,128)(2,1)}), bf16[2,16,132,96]{3,0,2,1:T(2,128)(2,1)}, u32[]{:S(2)}, u32[]{:S(2)}) async-start(bf16[2,16,132,96]{3,0,2,1:T(2,128)(2,1)} %copy.102), calls=%async_computation.4 | async-start | bytes 2162688 | tf_op jit(solution)/shard_map/all_to_all | solution.py:84
  210.9 0.0 copy-start
  210.9 4.0 %copy.106 = f32[2,132,1536]{2,0,1:T(2,128)} copy(f32[2,132,1536]{2,1,0:T(8,128)} %get-tuple-element.75) | data formatting | bytes 3244032
  214.9 0.0 copy-done
  214.9 2.4 %copy.107 = f32[2,132,1536]{2,0,1:T(2,128)} copy(f32[2,132,1536]{2,1,0:T(8,128)S(1)} %copy-done) | data formatting | bytes 3244032
  217.3 2.4 %copy.108 = f32[2,132,1536]{2,0,1:T(2,128)} copy(f32[2,132,1536]{2,1,0:T(8,128)S(1)} %get-tuple-element.77) | data formatting | bytes 3244032
  219.7 0.7 reshape.59
  220.5 3.0 %copy.113 = bf16[2,2,8,1,132,96]{4,2,1,5,0,3:T(8,128)(2,1)S(1)} copy(bf16[2,2,8,1,132,96]{5,1,2,4,0,3:T(2,128)(2,1)S(1)} %bitcast.40) | data formatting | bytes 1622016
  223.4 2.9 %reshape.61 = bf16[2,2112,96]{1,2,0:T(8,128)(2,1)} reshape(bf16[2,2,8,1,132,96]{4,2,1,5,0,3:T(8,128)(2,1)S(1)} %copy.113) | data formatting | bytes 1622016
  226.3 0.9 all-to-all-done.4
  227.3 2.3 multiply_bitcast_fusion
  229.6 0.4 copy.103
  230.0 2.3 mul.125
  232.3 2.4 %fusion.3 = f32[2,132,1536]{2,1,0:T(8,128)S(1)} fusion(f32[2,132,1536]{2,1,0:T(8,128)} %mul.125, f32[2,132,1536]{2,0,1:T(2,128)} %param.14), kind=kLoop, calls=%fused_computation.8 | loop fusion | flops 811008 | bytes 4866048 | tf_op jit(solution)/shard_map/add | solution.py:88
  234.7 2.4 %copy.109 = f32[2,132,1536]{2,0,1:T(2,128)} copy(f32[2,132,1536]{2,1,0:T(8,128)S(1)} %fusion.3) | data formatting | bytes 3244032
  (2 shorter events, 0.0 us)
Async XLA Ops:
  30.3 9.9 %copy-start.7 = (bf16[2,24]{1,0:T(2,128)(2,1)S(1)}, bf16[2,24]{1,0:T(2,128)(2,1)}, u32[]{:S(2)}) copy-start(bf16[2,24]{1,0:T(2,128)(2,1)} %param.15) | copy-start | bytes 292
  32.5 24.2 %all-to-all-start.1 = ((bf16[2,16,1,132,96]{4,0,3,2,1:T(2,128)(2,1)}), bf16[2,16,1,132,96]{4,0,3,2,1:T(2,128)(2,1)S(1)}, u32[]{:S(2)}, u32[]{:S(2)}) async-start(bf16[2,16,1,132,96]{4,0,3,2,1:T(2,128)(2,1)} %copy.90), calls=%async_computation.1 | async-start | bytes 2162688 | tf_op jit(solution)/shard_map/all_to_all | solution.py:53
  168.4 7.5 %copy-start.2 = (f32[2,24]{1,0:T(2,128)S(1)}, f32[2,24]{1,0:T(2,128)}, u32[]{:S(2)}) copy-start(f32[2,24]{1,0:T(2,128)} %param.19) | copy-start | bytes 580
  168.4 7.5 %copy-start.3 = (f32[2,24]{1,0:T(2,128)S(1)}, f32[2,24]{1,0:T(2,128)}, u32[]{:S(2)}) copy-start(f32[2,24]{1,0:T(2,128)} %param.16) | copy-start | bytes 580
  168.4 7.5 %copy-start.4 = (f32[2,24]{1,0:T(2,128)S(1)}, f32[2,24]{1,0:T(2,128)}, u32[]{:S(2)}) copy-start(f32[2,24]{1,0:T(2,128)} %param.17) | copy-start | bytes 580
  168.4 7.5 %copy-start.5 = (f32[2,24]{1,0:T(2,128)S(1)}, f32[2,24]{1,0:T(2,128)}, u32[]{:S(2)}) copy-start(f32[2,24]{1,0:T(2,128)} %param.18) | copy-start | bytes 580
  170.5 20.8 %all-to-all-start.3 = ((bf16[2,16,1,132,96]{4,0,3,2,1:T(2,128)(2,1)}), bf16[2,16,1,132,96]{4,0,3,2,1:T(2,128)(2,1)S(1)}, u32[]{:S(2)}, u32[]{:S(2)}) async-start(bf16[2,16,1,132,96]{4,0,3,2,1:T(2,128)(2,1)} %copy.97), calls=%async_computation.3 | async-start | bytes 2162688 | tf_op jit(solution)/shard_map/all_to_all | solution.py:72
  176.5 21.6 %copy-start.6 = (f32[2,24]{1,0:T(2,128)}, f32[2,24]{1,0:T(2,128)S(1)}, u32[]{:S(2)}) copy-start(f32[2,24]{1,0:T(2,128)S(1)} %get-tuple-element.71) | copy-start | bytes 580
  191.4 1.0 copy-start.1
  192.4 13.9 %all-to-all-start.5 = ((bf16[128,2,24]{2,1,0:T(2,128)(2,1)}), bf16[128,2,24]{2,1,0:T(2,128)(2,1)S(1)}, u32[]{:S(2)}, u32[]{:S(2)}) async-start(bf16[128,2,24]{2,1,0:T(2,128)(2,1)} %stack.2), calls=%async_computation.5 | async-start | bytes 131072 | tf_op jit(solution)/shard_map/all_to_all | solution.py:90
  206.3 21.0 %all-to-all-start.4 = ((bf16[2,16,132,96]{3,0,2,1:T(2,128)(2,1)}), bf16[2,16,132,96]{3,0,2,1:T(2,128)(2,1)}, u32[]{:S(2)}, u32[]{:S(2)}) async-start(bf16[2,16,132,96]{3,0,2,1:T(2,128)(2,1)} %copy.102), calls=%async_computation.4 | async-start | bytes 2162688 | tf_op jit(solution)/shard_map/all_to_all | solution.py:84
  210.9 4.0 %copy-start = (f32[2,132,1536]{2,1,0:T(8,128)S(1)}, f32[2,132,1536]{2,1,0:T(8,128)}, u32[]{:S(2)}) copy-start(f32[2,132,1536]{2,1,0:T(8,128)} %get-tuple-element.76) | copy-start | bytes 4866052
